TPU v7x, 32 devices: a whole 2x2x4 slice. The times are simulated.
32 devices in a mesh: rep: 2 (over x), shard: 16 (over z, y, core).
Axes of the slice: x: 2, y: 2, z: 4, core: 2. Of those that a mesh axis runs over, the one named last changes fastest.
Arguments:
- tokens: bfloat16 [32, 192, 2048], P(('rep', 'shard')), may hold values from -7 to 7
- segment_ids: int32 [32, 192], P(('rep', 'shard')), may hold values from 0 to 3, never falling along the last dimension, each value on 1 to 96 neighbouring positions
- norm_gain: bfloat16 [2048], P('shard'), may hold values from 0.25 to 1.75
- input_weight: bfloat16 [2048, 2048], P('shard'), may hold values from -0.125 to 0.125
- forget_weight: bfloat16 [2048, 2048], P('shard'), may hold values from -0.5 to 0.5
- gate_weight: bfloat16 [2048, 2048], P('shard'), may hold values from -0.125 to 0.125
- mixer_gain: bfloat16 [2048], P('shard'), may hold values from 0.25 to 1.75
- out_weight: bfloat16 [2048, 2048], P('shard'), may hold values from -0.1875 to 0.1875
- ffn_gain: bfloat16 [2048], P('shard'), may hold values from 0.25 to 1.75
- ffn_gate_weight: bfloat16 [2048, 5632], P('shard'), may hold values from -0.125 to 0.125
- ffn_up_weight: bfloat16 [2048, 5632], P('shard'), may hold values from -0.125 to 0.125
- ffn_down_weight: bfloat16 [5632, 2048], P('shard'), may hold values from -0.15625 to 0.15625
- cotangent: bfloat16 [32, 192, 2048], P(('rep', 'shard')), may hold values from -6 to 6
Outputs:
- block_output: bfloat16 [32, 192, 2048], P(('rep', 'shard'))
- input_grad: bfloat16 [32, 192, 2048], P(('rep', 'shard'))
- norm_gain_grad: float32 [2048], P('shard')
- input_weight_grad: float32 [2048, 2048], P('shard')
- forget_weight_grad: float32 [2048, 2048], P('shard')
- gate_weight_grad: float32 [2048, 2048], P('shard')
- mixer_gain_grad: float32 [2048], P('shard')
- out_weight_grad: float32 [2048, 2048], P('shard')
- ffn_gain_grad: float32 [2048], P('shard')
- ffn_gate_grad: float32 [2048, 5632], P('shard')
- ffn_up_grad: float32 [2048, 5632], P('shard')
- ffn_down_grad: float32 [5632, 2048], P('shard')
Inputs may be any that keep to these rules, and one draw needn't show every extreme that they name: `segment_ids`: document numbers never fall along a sequence; each document has 1 to 96 tokens, and one has exactly 96.
All inputs are finite; a program needn't handle non-finite values.
Results may differ from a plain program's by a relative error of at most 0.019.
Values may be sent and summed in bfloat16 or wider, within the bound.
No kernel may reach another device: no remote copies, remote signals or barrier semaphores. Data moves between devices by JAX's collectives and lax.ppermute only.
A program may use at most 640 MiB of HBM per device.

v0:
```python
import jax
import jax.numpy as jnp
from jax import lax
from jax.sharding import PartitionSpec as P

EPSILON = 1e-06


def normalize(values):
    scale = lax.rsqrt(jnp.mean(values * values, axis=-1, keepdims=True) + EPSILON)
    return (values * scale, scale)


def norm_back(grad_scaled, scaled, scale):
    inner = jnp.mean(grad_scaled * scaled, axis=-1, keepdims=True)
    return scale * (grad_scaled - scaled * inner)


def swish_pair(values):
    sigma = jax.nn.sigmoid(values)
    return (values * sigma, sigma * (1.0 + values * (1.0 - sigma)))


def combine_steps(earlier, later):
    return (earlier[0] * later[0], later[0] * earlier[1] + later[1])


def linear_scan(decay, update):
    return lax.associative_scan(combine_steps, (decay, update), axis=0)[1]


def contract_rows(left, piece):
    return lax.dot_general(
        left, piece, (((1,), (1,)), ((), ())), preferred_element_type=jnp.float32
    )


def gain_folder(scaled, carry, pieces):
    sums, fulls, gain_full = carry
    gain_piece = pieces[-1]
    matrices = pieces[:-1]
    columns = scaled * gain_piece.astype(jnp.float32)
    lowered = columns.astype(jnp.bfloat16)
    sums = tuple(
        (jnp.dot(lowered, piece, preferred_element_type=jnp.float32) for piece in matrices)
    )
    gain_full = gain_piece
    return (sums, fulls, gain_full)


def plain_folder(lowered_rows, carry, piece):
    total, full = carry
    total = jnp.dot(lowered_rows, piece, preferred_element_type=jnp.float32)
    return (total, full)


def start_carry(length, width, columns, number):
    sums = tuple((jnp.zeros((length, columns), jnp.float32) for index in range(number)))
    fulls = ()
    return (sums, fulls, jnp.zeros((width,), jnp.bfloat16))


def single_columns(left, piece):
    return contract_rows(left, piece)


def multi_columns(lefts, pieces):
    total = contract_rows(lefts[0], pieces[0])
    for left, piece in zip(lefts[1:], pieces[1:]):
        total = total + contract_rows(left, piece)
    return total


def row_grad(left, right):
    return lax.dot_general(
        left, right, (((0,), (0,)), ((), ())), preferred_element_type=jnp.float32
    )


def row_block(pairs, gains):
    pieces = [row_grad(left, right) for left, right in pairs]
    pieces = pieces + [vector[:, None] for vector in gains]
    return jnp.concatenate(pieces, axis=1)


def shards(
    tokens,
    segment_ids,
    norm_gain,
    input_weight,
    forget_weight,
    gate_weight,
    mixer_gain,
    out_weight,
    ffn_gain,
    ffn_gate_weight,
    ffn_up_weight,
    ffn_down_weight,
    cotangent,
):
    inputs = tokens[0].astype(jnp.float32)
    length, width = inputs.shape
    hidden_width = ffn_up_weight.shape[1]
    segments = segment_ids[0]
    same = jnp.concatenate(
        [jnp.zeros((1,), jnp.float32), (segments[1:] == segments[:-1]).astype(jnp.float32)]
    )
    scaled_in, scale_in = normalize(inputs)
    mixer_sums, mixer_full, gain_one = gain_folder(
        scaled_in,
        start_carry(length, width, width, 3),
        (
            lax.all_gather(input_weight, "shard", axis=0, tiled=True),
            lax.all_gather(forget_weight, "shard", axis=0, tiled=True),
            lax.all_gather(gate_weight, "shard", axis=0, tiled=True),
            lax.all_gather(norm_gain, "shard", axis=0, tiled=True),
        ),
    )
    input_pre, forget_pre, gate_pre = mixer_sums
    forget = jax.nn.sigmoid(forget_pre)
    input_act, input_slope = swish_pair(input_pre)
    update = input_act * (1.0 - forget)
    decay = forget * same[:, None]
    state = linear_scan(decay, update)
    state_scaled, state_scale = normalize(state)
    gate_act, gate_slope = swish_pair(gate_pre)
    mixed_pre = state_scaled * gate_act
    out_sums, out_full, gain_two = gain_folder(
        mixed_pre,
        start_carry(length, width, width, 1),
        (
            lax.all_gather(out_weight, "shard", axis=0, tiled=True),
            lax.all_gather(mixer_gain, "shard", axis=0, tiled=True),
        ),
    )
    resid = inputs + out_sums[0]
    scaled_mid, scale_mid = normalize(resid)
    ffn_sums, ffn_full, gain_three = gain_folder(
        scaled_mid,
        start_carry(length, width, hidden_width, 2),
        (
            lax.all_gather(ffn_gate_weight, "shard", axis=0, tiled=True),
            lax.all_gather(ffn_up_weight, "shard", axis=0, tiled=True),
            lax.all_gather(ffn_gain, "shard", axis=0, tiled=True),
        ),
    )
    ffn_gate, ffn_up = ffn_sums
    ffn_act, ffn_slope = swish_pair(ffn_gate)
    hidden = (ffn_act * ffn_up).astype(jnp.bfloat16)
    down_start = (jnp.zeros((length, width), jnp.float32), jnp.zeros((1, 1), jnp.bfloat16))
    ffn_out, down_full = plain_folder(
        hidden, down_start, lax.all_gather(ffn_down_weight, "shard", axis=0, tiled=True)
    )
    block_output = (resid + ffn_out).astype(jnp.bfloat16)
    grad_out = cotangent[0]
    grad_hidden = single_columns(
        grad_out, lax.all_gather(ffn_down_weight, "shard", axis=0, tiled=True)
    )
    grad_fgate = (grad_hidden * ffn_up * ffn_slope).astype(jnp.bfloat16)
    grad_fup = (grad_hidden * ffn_act).astype(jnp.bfloat16)
    grad_ffn_in = multi_columns(
        (grad_fgate, grad_fup),
        lax.all_gather((ffn_gate_weight, ffn_up_weight), "shard", axis=0, tiled=True),
    )
    gain_three_f = gain_three.astype(jnp.float32)
    mid_low = (scaled_mid * gain_three_f).astype(jnp.bfloat16)
    gain_three_grad = jnp.sum(grad_ffn_in * scaled_mid, axis=0)
    grad_resid = grad_out.astype(jnp.float32) + norm_back(
        grad_ffn_in * gain_three_f, scaled_mid, scale_mid
    )
    grad_branch = grad_resid.astype(jnp.bfloat16)
    grad_mixed = single_columns(
        grad_branch, lax.all_gather(out_weight, "shard", axis=0, tiled=True)
    )
    gain_two_f = gain_two.astype(jnp.float32)
    mixed_low = (mixed_pre * gain_two_f).astype(jnp.bfloat16)
    gain_two_grad = jnp.sum(grad_mixed * mixed_pre, axis=0)
    weighted = grad_mixed * gain_two_f
    grad_gate_pre = (weighted * state_scaled * gate_slope).astype(jnp.bfloat16)
    grad_state = norm_back(weighted * gate_act, state_scaled, state_scale)
    next_decay = jnp.concatenate([decay[1:], jnp.zeros((1, width), jnp.float32)])
    carried = jnp.flip(linear_scan(jnp.flip(next_decay, 0), jnp.flip(grad_state, 0)), 0)
    previous = jnp.concatenate([jnp.zeros((1, width), jnp.float32), state[:-1]])
    grad_forget = carried * previous * same[:, None] - carried * input_act
    grad_input_pre = (carried * (1.0 - forget) * input_slope).astype(jnp.bfloat16)
    grad_forget_pre = (grad_forget * forget * (1.0 - forget)).astype(jnp.bfloat16)
    triple = (grad_input_pre, grad_forget_pre, grad_gate_pre)
    grad_normed = multi_columns(
        triple,
        lax.all_gather((input_weight, forget_weight, gate_weight), "shard", axis=0, tiled=True),
    )
    gain_one_f = gain_one.astype(jnp.float32)
    in_low = (scaled_in * gain_one_f).astype(jnp.bfloat16)
    gain_one_grad = jnp.sum(grad_normed * scaled_in, axis=0)
    input_grad = (grad_resid + norm_back(grad_normed * gain_one_f, scaled_in, scale_in)).astype(
        jnp.bfloat16
    )
    triple_joined = jnp.concatenate(triple, axis=1)
    pair_joined = jnp.concatenate([grad_fgate, grad_fup], axis=1)
    pairs = ((in_low, triple_joined), (mixed_low, grad_branch), (mid_low, pair_joined))
    gains = (gain_one_grad, gain_two_grad, gain_three_grad)
    rows_term = lax.psum_scatter(
        row_block(pairs, gains).astype(jnp.bfloat16), "shard", scatter_dimension=0, tiled=True
    )
    down_term = lax.psum_scatter(
        row_grad(hidden, grad_out).astype(jnp.bfloat16), "shard", scatter_dimension=0, tiled=True
    )
    rows_total, down_total = (
        lax.psum(rows_term, "rep").astype(jnp.float32),
        lax.psum(down_term, "rep").astype(jnp.float32),
    )
    tail = 4 * width + 2 * hidden_width
    return (
        block_output[None],
        input_grad[None],
        rows_total[:, tail],
        rows_total[:, :width],
        rows_total[:, width : 2 * width],
        rows_total[:, 2 * width : 3 * width],
        rows_total[:, tail + 1],
        rows_total[:, 3 * width : 4 * width],
        rows_total[:, tail + 2],
        rows_total[:, 4 * width : 4 * width + hidden_width],
        rows_total[:, 4 * width + hidden_width : tail],
        down_total,
    )


def solution(mesh):
    placed = (
        P(("rep", "shard"), None, None),
        P(("rep", "shard"), None),
        P("shard"),
        P("shard", None),
        P("shard", None),
        P("shard", None),
        P("shard"),
        P("shard", None),
        P("shard"),
        P("shard", None),
        P("shard", None),
        P("shard", None),
        P(("rep", "shard"), None, None),
    )
    return jax.shard_map(
        shards,
        mesh=mesh,
        in_specs=placed,
        out_specs=(
            P(("rep", "shard"), None, None),
            P(("rep", "shard"), None, None),
            P("shard"),
            P("shard", None),
            P("shard", None),
            P("shard", None),
            P("shard"),
            P("shard", None),
            P("shard"),
            P("shard", None),
            P("shard", None),
            P("shard", None),
        ),
        check_vma=False,
    )
```

profile of v0, /device:TPU:0, one launch (start us, length us, event | category | flops | bytes accessed | tf_op | source)
XLA Modules:
  0.0 2012.6 jit_solution(17651145178794768228)
XLA Ops:
  12.0 23.2 %all-gather = bf16[16,1,128]{2,1,0:T(2,128)(2,1)S(1)} all-gather(bf16[1,1,128]{2,1,0:T(2,128)(2,1)S(1)} %bitcast.75), channel_id=1, replica_groups=mesh['rep'=2,'shard'=16] {'shard'}, dimensions={0}, use_global_device_ids=true | all-gather | bytes 4352 | tf_op jit(solution)/shard_map/all_gather | solution.py:116
  35.2 17.5 all-gather.1
  52.7 18.9 all-gather.2
  72.6 15.3 all-gather.11.cloned.1.call-done
  87.9 6.4 fusion.57
  94.3 69.0 %all-gather.13.cloned.1.call-done = bf16[2048,2048]{1,0:T(8,128)(2,1)} async-done(((bf16[128,2048]{1,0:T(8,128)(2,1)}), bf16[2048,2048]{1,0:T(8,128)(2,1)}) %all-gather.13.cloned.1.call-update) | async-done | bytes 8388624 | tf_op jit(solution)/shard_map/all_gather | solution.py:114
  163.3 7.8 broadcast_multiply_fusion
  177.4 4.4 slice.444
  200.5 38.1 %all-gather.15.cloned.1.call-done = bf16[2048,2048]{1,0:T(8,128)(2,1)} async-done(((bf16[128,2048]{1,0:T(8,128)(2,1)}), bf16[2048,2048]{1,0:T(8,128)(2,1)}) %all-gather.15.cloned.1.call-update) | async-done | bytes 8388624 | tf_op jit(solution)/shard_map/all_gather | solution.py:115
  238.6 7.6 multiply_multiply_fusion.1
  246.2 67.6 %all-gather.17.cloned.1.call-done = bf16[2048,2048]{1,0:T(8,128)(2,1)} async-done(((bf16[128,2048]{1,0:T(8,128)(2,1)}), bf16[2048,2048]{1,0:T(8,128)(2,1)}) %all-gather.17.cloned.1.call-update) | async-done | bytes 8388624 | tf_op jit(solution)/shard_map/all_gather | solution.py:132
  313.8 5.9 multiply_reduce_fusion.4
  322.0 110.3 %all-gather.21.cloned.1.call-done = bf16[2048,5632]{1,0:T(8,128)(2,1)} async-done(((bf16[128,5632]{1,0:T(8,128)(2,1)}), bf16[2048,5632]{1,0:T(8,128)(2,1)}) %all-gather.21.cloned.1.call-update) | async-done | bytes 23068688 | tf_op jit(solution)/shard_map/all_gather | solution.py:143
  432.3 14.5 fusion.74
  446.8 105.7 %all-gather.19.cloned.1.call-done = bf16[2048,5632]{1,0:T(8,128)(2,1)} async-done(((bf16[128,5632]{1,0:T(8,128)(2,1)}), bf16[2048,5632]{1,0:T(8,128)(2,1)}) %all-gather.19.cloned.1.call-update) | async-done | bytes 23068688 | tf_op jit(solution)/shard_map/all_gather | solution.py:142
  552.4 14.7 fusion.73
  567.1 105.7 %all-gather.23.cloned.1.call-done = bf16[5632,2048]{1,0:T(8,128)(2,1)} async-done(((bf16[352,2048]{1,0:T(8,128)(2,1)}), bf16[5632,2048]{1,0:T(8,128)(2,1)}) %all-gather.23.cloned.1.call-update) | async-done | bytes 23068688 | tf_op jit(solution)/shard_map/all_gather | solution.py:152
  672.8 16.0 multiply_convert_fusion
  690.1 10.9 convolution_convert_fusion.1
  703.9 4.4 slice.456
  708.3 4.5 slice.449
  712.8 4.5 slice.447
  717.3 8.6 slice.457
  725.9 8.7 slice.448
  734.6 8.6 slice.450
  745.4 12.1 fusion.75
  757.6 14.4 multiply_reduce_fusion
  775.2 8.6 multiply_reduce_fusion.1
  791.4 8.6 slice.452
  800.1 5.1 slice.454
  824.8 5.5 slice.504
  838.6 5.2 pad.115
  846.6 16.0 rev.6
  862.6 4.1 multiply_convert_fusion.4
  866.8 6.8 fusion.76
  873.7 2.9 convolution_add_fusion.1
  876.7 4.3 fusion.24
  882.1 5.8 convolution_convert_fusion.3
  887.9 12.3 copy.30
  900.2 13.6 convolution_convert_fusion.2
  913.7 20.9 %convolution_convert_fusion = bf16[2048,11264]{1,0:T(8,128)(2,1)} fusion(bf16[192,2048]{1,0:T(8,128)(2,1)} %multiply_convert_fusion.6, bf16[192,5632]{1,0:T(8,128)(2,1)} %get-tuple-element.29, bf16[192,5632]{1,0:T(8,128)(2,1)} %get-tuple-element.30), kind=kOutput, calls=%fused_computation | convolution fusion | flops 8890089472 | bytes 51249152 | tf_op jit(solution)/shard_map/dot_general | solution.py:75
  934.6 158.1 %concatenate.84 = bf16[2048,19459]{1,0:T(8,128)(2,1)} concatenate(bf16[2048,6144]{1,0:T(8,128)(2,1)} %convolution_convert_fusion.2, bf16[2048,2048]{1,0:T(8,128)(2,1)} %copy.30, bf16[2048,11264]{1,0:T(8,128)(2,1)} %convolution_convert_fusion, bf16[2048,1]{1,0:T(8,128)(2,1)} %broadcast_in_dim.18, bf16[2048,1]{1,0:T(8,128)(2,1)S(1)} %copy-done.24, bf16[2048,1]{1,0:T(8,128)(2,1)S(1)} %copy-done.25), dimensions={1} | concatenate | bytes 159408128 | tf_op jit(solution)/shard_map/concatenate | solution.py:83
  1092.8 743.0 %reduce-scatter.3.cloned.1.call-done = bf16[128,19459]{1,0:T(8,128)(2,1)} async-done(((bf16[2048,19459]{1,0:T(8,128)(2,1)}), bf16[128,19459]{1,0:T(8,128)(2,1)}) %reduce-scatter.3.cloned.1.call-update) | async-done | bytes 4981520 | tf_op jit(solution)/shard_map/reduce_scatter | solution.py:202
  1835.9 2.9 fusion.28
  1838.7 12.3 fusion.8
  1851.0 143.4 %all-reduce.33.cloned.1.call-done = (bf16[128,19459]{1,0:T(8,128)(2,1)}, bf16[352,2048]{1,0:T(8,128)(2,1)}) async-done(((bf16[128,19459]{1,0:T(8,128)(2,1)}, bf16[352,2048]{1,0:T(8,128)(2,1)}), (bf16[128,19459]{1,0:T(8,128)(2,1)}, bf16[352,2048]{1,0:T(8,128)(2,1)})) %all-reduce.33.cloned.1.call-update) | async-done | bytes 6423312 | tf_op jit(solution)/shard_map/psum | solution.py:209
  1994.4 3.8 fusion.60
  1998.3 3.2 fusion.59
  (310 shorter events, 85.3 us)
Async XLA Ops:
  7.2 80.7 %all-gather.11.cloned.1.call-start = ((), (), s32[]{:S(2)}) async-start(), calls=%async_computation.2 | async-start | bytes 8912896 | tf_op jit(solution)/shard_map/all_gather | solution.py:113
  7.9 155.3 %all-gather.13.cloned.1.call-start = ((), (), s32[]{:S(2)}) async-start(), calls=%async_computation.3 | async-start | bytes 8912896 | tf_op jit(solution)/shard_map/all_gather | solution.py:114
  8.7 229.9 %all-gather.15.cloned.1.call-start = ((), (), s32[]{:S(2)}) async-start(), calls=%async_computation.4 | async-start | bytes 8912896 | tf_op jit(solution)/shard_map/all_gather | solution.py:115
  9.4 304.4 %all-gather.17.cloned.1.call-start = ((), (), s32[]{:S(2)}) async-start(), calls=%async_computation.5 | async-start | bytes 8912896 | tf_op jit(solution)/shard_map/all_gather | solution.py:132
  10.0 422.3 %all-gather.21.cloned.1.call-start = ((), (), s32[]{:S(2)}) async-start(), calls=%async_computation.7 | async-start | bytes 24510464 | tf_op jit(solution)/shard_map/all_gather | solution.py:143
  10.6 24.7 %copy-start.46 = (bf16[128]{0:T(256)(128)(2,1)S(1)}, bf16[128]{0:T(256)(128)(2,1)}, u32[]{:S(2)}) copy-start(bf16[128]{0:T(256)(128)(2,1)} %param.19) | copy-start | bytes 772
  10.6 42.1 %copy-start.47 = (bf16[128]{0:T(256)(128)(2,1)S(1)}, bf16[128]{0:T(256)(128)(2,1)}, u32[]{:S(2)}) copy-start(bf16[128]{0:T(256)(128)(2,1)} %param.21) | copy-start | bytes 772
  10.6 61.6 %copy-start.44 = (s32[1,192]{1,0:T(1,128)S(1)}, s32[1,192]{1,0:T(1,128)}, u32[]{:S(2)}) copy-start(s32[1,192]{1,0:T(1,128)} %param.14) | copy-start | bytes 2308
  10.6 61.8 %copy-start.1 = (bf16[1,192,2048]{2,1,0:T(8,128)(2,1)S(1)}, bf16[1,192,2048]{2,1,0:T(8,128)(2,1)}, u32[]{:S(2)}) copy-start(bf16[1,192,2048]{2,1,0:T(8,128)(2,1)} %param.13) | copy-start | bytes 2359300
  10.6 541.8 %all-gather.19.cloned.1.call-start = ((), (), s32[]{:S(2)}) async-start(), calls=%async_computation.6 | async-start | bytes 24510464 | tf_op jit(solution)/shard_map/all_gather | solution.py:142
  11.2 661.6 %all-gather.23.cloned.1.call-start = ((), (), s32[]{:S(2)}) async-start(), calls=%async_computation.8 | async-start | bytes 24510464 | tf_op jit(solution)/shard_map/all_gather | solution.py:152
  11.9 1080.8 %reduce-scatter.5.cloned.1.call-start = ((), (), s32[]{:S(2)}) async-start(), calls=%async_computation.10 | async-start | bytes 24510464 | tf_op jit(solution)/shard_map/reduce_scatter | solution.py:205
  72.4 90.9 %copy-start.42 = (f32[192]{0:T(256)}, f32[192]{0:T(256)S(1)}, u32[]{:S(2)}) copy-start(f32[192]{0:T(256)S(1)} %add_convert_fusion) | copy-start | bytes 2308
  72.6 90.6 %copy-start.32 = (f32[192]{0:T(256)}, f32[192]{0:T(256)S(1)}, u32[]{:S(2)}) copy-start(f32[192]{0:T(256)S(1)} %add_rsqrt_fusion.2) | copy-start | bytes 2308
  171.0 2.6 copy-start.3
  175.9 6.0 copy-start.10
  181.9 4.3 copy-start.13
  194.1 1.6 copy-start.18
  199.1 39.5 %copy-start.33 = (f32[192]{0:T(256)S(1)}, f32[192]{0:T(256)}, u32[]{:S(2)}) copy-start(f32[192]{0:T(256)} %copy-done.32) | copy-start | bytes 2308
  313.8 7.1 copy-start.31
  672.8 17.3 copy-start.20
  701.1 1134.7 %reduce-scatter.3.cloned.1.call-start = ((), (), s32[]{:S(2)}) async-start(), calls=%async_computation.9 | async-start | bytes 85229568 | tf_op jit(solution)/shard_map/reduce_scatter | solution.py:202
  743.2 2.2 copy-start.23
  745.4 12.2 copy-start.6
  772.0 2.2 copy-start.4
  772.0 2.7 copy-start.21
  772.0 3.2 copy-start.27
  791.4 8.7 copy-start.15
  810.3 3.6 copy-start.26
  819.0 5.8 copy-start.14
  822.9 7.7 copy-start.41
  832.9 1.7 copy-start.19
  846.6 16.0 copy-start.43
  862.6 11.0 slice-start
  866.8 6.9 copy-start.12
  866.8 6.9 slice-start.1
  866.8 9.8 slice-start.2
  873.7 2.9 copy-start.2
  873.7 2.9 slice-start.3
  873.7 2.9 copy-start.11
  873.7 2.9 copy-start.34
  876.6 5.4 copy-start.22
  913.7 20.9 %copy-start.24 = (bf16[2048,1]{1,0:T(8,128)(2,1)S(1)}, bf16[2048,1]{1,0:T(8,128)(2,1)}, u32[]{:S(2)}) copy-start(bf16[2048,1]{1,0:T(8,128)(2,1)} %broadcast_in_dim.19) | copy-start | bytes 12292
  913.7 20.9 %copy-start.25 = (bf16[2048,1]{1,0:T(8,128)(2,1)S(1)}, bf16[2048,1]{1,0:T(8,128)(2,1)}, u32[]{:S(2)}) copy-start(bf16[2048,1]{1,0:T(8,128)(2,1)} %broadcast_in_dim.20) | copy-start | bytes 12292
  1092.7 901.7 %all-reduce.33.cloned.1.call-start = ((), (), s32[]{:S(2)}) async-start(), calls=%async_computation.11 | async-start | bytes 12910592 | tf_op jit(solution)/shard_map/psum | solution.py:209
  1835.8 2.9 copy-start.7
  1835.9 2.9 copy-start.9
  1994.4 3.9 copy-start
  (14 other events, 14.5 us)
Sparse Core Ops, SparseCore 0:
  10.2 77.6 all-gather.10
  90.1 73.1 all-gather.12
  165.4 73.1 all-gather.14
  240.6 73.1 all-gather.16
  315.3 116.9 all-gather.20
  433.7 118.6 all-gather.18
  554.0 118.6 all-gather.22
  701.2 226.8 reduce-scatter.4
  1092.8 742.9 reduce-scatter.2
  1838.2 156.2 all-reduce.32
where the time goes:
time: 2030 us; the launch traced here: 2010 us
  waiting for transfers between devices  1400 us (69%)
  local copies, waits for them, and re-layouts  319 us (16%)
  matrix products  185 us (9%)
  blocking collectives  59.6 us (3%)
  other arithmetic  30.4 us (1%)
    reduce_scatter x1, waiting for transfers between devices, shards(): lax.psum_scatter(row_block(pairs, gains).astype(jnp.bfloat16), 'shard', s...  743 us
    concatenate x1, local copies, waits for them, and re-layouts, row_block(): return jnp.concatenate(pieces, axis=1)  158 us
    psum x1, waiting for transfers between devices, shards(): lax.psum(rows_term, 'rep').astype(jnp.float32)  143 us
    all_gather x1, waiting for transfers between devices, shards(): lax.all_gather(ffn_up_weight, 'shard', axis=0, tiled=True)  110 us
    all_gather x1, waiting for transfers between devices, shards(): lax.all_gather(ffn_gate_weight, 'shard', axis=0, tiled=True)  106 us
    all_gather x1, waiting for transfers between devices, shards(): lax.all_gather(ffn_down_weight, 'shard', axis=0, tiled=True)  106 us
    slice x90, local copies, waits for them, and re-layouts, linear_scan(): return lax.associative_scan(combine_steps, (decay, update), axis=0)[1]  96.4 us
    all_gather x1, waiting for transfers between devices, shards(): lax.all_gather(forget_weight, 'shard', axis=0, tiled=True)  69 us
  transfers between devices with their start and end apart: 10, of which 9 were waited for; matrix products, arithmetic and copies ran while one was open for 24% of the time, Pallas kernels for 0%

commit v1 on v0

--- a/solution.py
+++ b/solution.py
@@ -4,6 +4,33 @@
 from jax.sharding import PartitionSpec as P
 
 EPSILON = 1e-06
+
+
+def array_refer(w_in, on_dim):
+    everything = list(w_in.shape[1:])
+    everything[on_dim] *= w_in.shape[0]
+    return jnp.moveaxis(w_in, 0, on_dim).reshape(everything)
+
+
+def patch_make(page, link_axis):
+    local_out = lax.psum(1, link_axis)
+    plain = lax.axis_index(link_axis)
+    y2, arr_next = (local_out, plain)
+    right_arr, current_value = (page[None], 1)
+    while current_value < y2:
+        opened = tuple(((to_i, to_i ^ current_value) for to_i in range(y2)))
+        w2 = lax.ppermute(right_arr, link_axis, opened)
+        piece_out = arr_next & current_value == 0
+        block_now = jnp.where(piece_out, right_arr, w2)
+        extra = jnp.where(piece_out, w2, right_arr)
+        right_arr = jnp.concatenate([block_now, extra])
+        current_value *= 2
+    return right_arr
+
+
+def search_leaves_in(s0, frame, d0):
+    e_next = patch_make(s0, frame)
+    return array_refer(e_next, d0)
 
 
 def normalize(values):
@@ -149,7 +176,7 @@
     hidden = (ffn_act * ffn_up).astype(jnp.bfloat16)
     down_start = (jnp.zeros((length, width), jnp.float32), jnp.zeros((1, 1), jnp.bfloat16))
     ffn_out, down_full = plain_folder(
-        hidden, down_start, lax.all_gather(ffn_down_weight, "shard", axis=0, tiled=True)
+        hidden, down_start, search_leaves_in(ffn_down_weight, "shard", 0)
     )
     block_output = (resid + ffn_out).astype(jnp.bfloat16)
     grad_out = cotangent[0]

time: 2030 us -> 2470 us (1.22)
  waiting for transfers between devices: 1400 us -> 1780 us
  other arithmetic: 30.4 us -> 86.2 us
    ppermute x0 -> x4, waiting for transfers between devices: none -> 318 us  [patch_make(): w2 = lax.ppermute(right_arr, link_axis, opened)]
    reduce_scatter x1, waiting for transfers between devices: 743 us -> 840 us  [shards(): lax.psum_scatter(row_block(pairs, gains).astype(jnp.bfloat16), 'shard', s...]
    psum x1, waiting for transfers between devices: 143 us -> 107 us  [shards(): lax.psum(rows_term, 'rep').astype(jnp.float32)]
    concatenate x0 -> x4, other arithmetic: none -> 31.5 us  [patch_make(): right_arr = jnp.concatenate([block_now, extra])]
    select_n x0 -> x4, other arithmetic: none -> 25.8 us  [patch_make(): block_now = jnp.where(piece_out, right_arr, w2)]
  transfers between devices with their start and end apart: 10 -> 14, of which waited for: 9 -> 12; matrix products, arithmetic and copies ran while one was open for 24% -> 22% of each run, Pallas kernels for 0% -> 0%
where the time goes in v1:
time: 2470 us; the launch traced here: 2460 us
  waiting for transfers between devices  1780 us (72%)
  local copies, waits for them, and re-layouts  325 us (13%)
  matrix products  184 us (7%)
  other arithmetic  86.2 us (3%)
  blocking collectives  59.6 us (2%)
    reduce_scatter x1, waiting for transfers between devices, shards(): lax.psum_scatter(row_block(pairs, gains).astype(jnp.bfloat16), 'shard', s...  840 us
    ppermute x4, waiting for transfers between devices, patch_make(): w2 = lax.ppermute(right_arr, link_axis, opened)  318 us
    concatenate x1, local copies, waits for them, and re-layouts, row_block(): return jnp.concatenate(pieces, axis=1)  158 us
    all_gather x1, waiting for transfers between devices, shards(): lax.all_gather(ffn_up_weight, 'shard', axis=0, tiled=True)  110 us
    psum x1, waiting for transfers between devices, shards(): lax.psum(rows_term, 'rep').astype(jnp.float32)  107 us
    all_gather x1, waiting for transfers between devices, shards(): lax.all_gather(ffn_gate_weight, 'shard', axis=0, tiled=True)  106 us
    all_gather x1, waiting for transfers between devices, shards(): lax.all_gather(ffn_down_weight, 'shard', axis=0, tiled=True)  106 us
    slice x90, local copies, waits for them, and re-layouts, linear_scan(): return lax.associative_scan(combine_steps, (decay, update), axis=0)[1]  96.5 us
  transfers between devices with their start and end apart: 14, of which 12 were waited for; matrix products, arithmetic and copies ran while one was open for 22% of the time, Pallas kernels for 0%

profile of v1, /device:TPU:0, one launch (start us, length us, event | category | flops | bytes accessed | tf_op | source)
XLA Modules:
  0.0 2458.2 jit_solution(6857953637173491173)
XLA Ops:
  12.0 23.2 all-gather
  35.2 17.5 all-gather.1
  52.7 18.9 all-gather.2
  72.6 15.3 all-gather.11.cloned.1.call-done
  87.9 6.4 fusion.57
  94.3 69.0 %all-gather.13.cloned.1.call-done = bf16[2048,2048]{1,0:T(8,128)(2,1)} async-done(((bf16[128,2048]{1,0:T(8,128)(2,1)}), bf16[2048,2048]{1,0:T(8,128)(2,1)}) %all-gather.13.cloned.1.call-update) | async-done | bytes 8388624 | tf_op jit(solution)/shard_map/all_gather | solution.py:141
  163.3 7.8 broadcast_multiply_fusion
  177.4 4.4 slice.444
  200.5 38.1 %all-gather.15.cloned.1.call-done = bf16[2048,2048]{1,0:T(8,128)(2,1)} async-done(((bf16[128,2048]{1,0:T(8,128)(2,1)}), bf16[2048,2048]{1,0:T(8,128)(2,1)}) %all-gather.15.cloned.1.call-update) | async-done | bytes 8388624 | tf_op jit(solution)/shard_map/all_gather | solution.py:142
  238.6 7.8 multiply_multiply_fusion.1
  246.4 67.5 %all-gather.17.cloned.1.call-done = bf16[2048,2048]{1,0:T(8,128)(2,1)} async-done(((bf16[128,2048]{1,0:T(8,128)(2,1)}), bf16[2048,2048]{1,0:T(8,128)(2,1)}) %all-gather.17.cloned.1.call-update) | async-done | bytes 8388624 | tf_op jit(solution)/shard_map/all_gather | solution.py:159
  313.8 6.0 multiply_reduce_fusion.4
  322.1 110.2 %all-gather.21.cloned.1.call-done = bf16[2048,5632]{1,0:T(8,128)(2,1)} async-done(((bf16[128,5632]{1,0:T(8,128)(2,1)}), bf16[2048,5632]{1,0:T(8,128)(2,1)}) %all-gather.21.cloned.1.call-update) | async-done | bytes 23068688 | tf_op jit(solution)/shard_map/all_gather | solution.py:170
  432.3 14.4 fusion.74
  446.7 105.7 %all-gather.19.cloned.1.call-done = bf16[2048,5632]{1,0:T(8,128)(2,1)} async-done(((bf16[128,5632]{1,0:T(8,128)(2,1)}), bf16[2048,5632]{1,0:T(8,128)(2,1)}) %all-gather.19.cloned.1.call-update) | async-done | bytes 23068688 | tf_op jit(solution)/shard_map/all_gather | solution.py:169
  552.5 14.7 fusion.73
  567.1 105.7 %all-gather.23.cloned.1.call-done = bf16[5632,2048]{1,0:T(8,128)(2,1)} async-done(((bf16[352,2048]{1,0:T(8,128)(2,1)}), bf16[5632,2048]{1,0:T(8,128)(2,1)}) %all-gather.23.cloned.1.call-update) | async-done | bytes 23068688 | tf_op jit(solution)/shard_map/all_gather | solution.py:184
  672.8 16.0 multiply_convert_fusion
  690.2 10.8 convolution_convert_fusion.1
  703.8 4.4 slice.456
  708.2 4.5 slice.449
  712.8 4.5 slice.447
  717.2 8.6 slice.457
  725.9 8.7 slice.448
  734.5 8.6 slice.450
  745.3 12.1 fusion.75
  757.5 14.4 multiply_reduce_fusion
  775.2 8.6 multiply_reduce_fusion.1
  791.5 8.7 slice.452
  800.1 5.1 slice.454
  824.8 5.5 slice.504
  838.7 5.4 pad.115
  846.9 16.1 rev.6
  867.2 6.8 fusion.76
  882.4 5.8 convolution_convert_fusion.3
  888.2 12.4 copy.30
  900.7 12.3 convolution_convert_fusion.2
  913.0 20.9 convolution_convert_fusion
  933.9 157.9 %concatenate.100 = bf16[2048,19459]{1,0:T(8,128)(2,1)} concatenate(bf16[2048,6144]{1,0:T(8,128)(2,1)} %convolution_convert_fusion.2, bf16[2048,2048]{1,0:T(8,128)(2,1)} %copy.30, bf16[2048,11264]{1,0:T(8,128)(2,1)} %convolution_convert_fusion, bf16[2048,1]{1,0:T(8,128)(2,1)S(1)} %copy-done.38, bf16[2048,1]{1,0:T(8,128)(2,1)S(1)} %copy-done.36, bf16[2048,1]{1,0:T(8,128)(2,1)S(1)} %copy-done.37), dimensions={1} | concatenate | bytes 159408128 | tf_op jit(solution)/shard_map/concatenate | solution.py:110
  1099.5 63.4 %collective-permute-done.1 = bf16[2,352,2048]{2,1,0:T(8,128)(2,1)} collective-permute-done((bf16[2,352,2048]{2,1,0:T(8,128)(2,1)S(1)}, bf16[2,352,2048]{2,1,0:T(8,128)(2,1)}, u32[]{:S(2)}, u32[]{:S(2)}) %collective-permute-start.1) | collective-permute-done | bytes 2883616 | tf_op jit(solution)/shard_map/ppermute | solution.py:22
  1173.7 251.8 %collective-permute-done.2 = bf16[4,352,2048]{2,1,0:T(8,128)(2,1)} collective-permute-done((bf16[4,352,2048]{2,1,0:T(8,128)(2,1)}, bf16[4,352,2048]{2,1,0:T(8,128)(2,1)}, u32[]{:S(2)}, u32[]{:S(2)}) %collective-permute-start.2) | collective-permute-done | bytes 5767200 | tf_op jit(solution)/shard_map/ppermute | solution.py:22
  1425.5 4.3 broadcast_select_fusion.3
  1429.8 6.7 pad_maximum_fusion.1
  1441.1 839.7 %reduce-scatter.3.cloned.1.call-done = bf16[128,19459]{1,0:T(8,128)(2,1)} async-done(((bf16[2048,19459]{1,0:T(8,128)(2,1)}), bf16[128,19459]{1,0:T(8,128)(2,1)}) %reduce-scatter.3.cloned.1.call-update) | async-done | bytes 4981520 | tf_op jit(solution)/shard_map/reduce_scatter | solution.py:229
  2280.8 17.0 broadcast_select_fusion.1
  2297.8 20.8 pad_maximum_fusion
  2321.0 11.6 fusion.8
  2332.6 107.4 %all-reduce.33.cloned.1.call-done = (bf16[128,19459]{1,0:T(8,128)(2,1)}, bf16[352,2048]{1,0:T(8,128)(2,1)}) async-done(((bf16[128,19459]{1,0:T(8,128)(2,1)}, bf16[352,2048]{1,0:T(8,128)(2,1)}), (bf16[128,19459]{1,0:T(8,128)(2,1)}, bf16[352,2048]{1,0:T(8,128)(2,1)})) %all-reduce.33.cloned.1.call-update) | async-done | bytes 6423312 | tf_op jit(solution)/shard_map/psum | solution.py:236
  (352 shorter events, 129.2 us)
Async XLA Ops:
  7.2 80.7 %all-gather.11.cloned.1.call-start = ((), (), s32[]{:S(2)}) async-start(), calls=%async_computation.2 | async-start | bytes 8912896 | tf_op jit(solution)/shard_map/all_gather | solution.py:140
  7.9 155.3 %all-gather.13.cloned.1.call-start = ((), (), s32[]{:S(2)}) async-start(), calls=%async_computation.3 | async-start | bytes 8912896 | tf_op jit(solution)/shard_map/all_gather | solution.py:141
  8.7 229.9 %all-gather.15.cloned.1.call-start = ((), (), s32[]{:S(2)}) async-start(), calls=%async_computation.4 | async-start | bytes 8912896 | tf_op jit(solution)/shard_map/all_gather | solution.py:142
  9.4 304.4 %all-gather.17.cloned.1.call-start = ((), (), s32[]{:S(2)}) async-start(), calls=%async_computation.5 | async-start | bytes 8912896 | tf_op jit(solution)/shard_map/all_gather | solution.py:159
  10.0 422.3 %all-gather.21.cloned.1.call-start = ((), (), s32[]{:S(2)}) async-start(), calls=%async_computation.7 | async-start | bytes 24510464 | tf_op jit(solution)/shard_map/all_gather | solution.py:170
  10.6 24.7 %copy-start.59 = (bf16[128]{0:T(256)(128)(2,1)S(1)}, bf16[128]{0:T(256)(128)(2,1)}, u32[]{:S(2)}) copy-start(bf16[128]{0:T(256)(128)(2,1)} %param.19) | copy-start | bytes 772
  10.6 42.1 %copy-start.60 = (bf16[128]{0:T(256)(128)(2,1)S(1)}, bf16[128]{0:T(256)(128)(2,1)}, u32[]{:S(2)}) copy-start(bf16[128]{0:T(256)(128)(2,1)} %param.21) | copy-start | bytes 772
  10.6 61.6 %copy-start.57 = (s32[1,192]{1,0:T(1,128)S(1)}, s32[1,192]{1,0:T(1,128)}, u32[]{:S(2)}) copy-start(s32[1,192]{1,0:T(1,128)} %param.14) | copy-start | bytes 2308
  10.6 61.8 %copy-start.8 = (bf16[1,192,2048]{2,1,0:T(8,128)(2,1)S(1)}, bf16[1,192,2048]{2,1,0:T(8,128)(2,1)}, u32[]{:S(2)}) copy-start(bf16[1,192,2048]{2,1,0:T(8,128)(2,1)} %param.13) | copy-start | bytes 2359300
  10.6 541.8 %all-gather.19.cloned.1.call-start = ((), (), s32[]{:S(2)}) async-start(), calls=%async_computation.6 | async-start | bytes 24510464 | tf_op jit(solution)/shard_map/all_gather | solution.py:169
  11.2 661.6 %all-gather.23.cloned.1.call-start = ((), (), s32[]{:S(2)}) async-start(), calls=%async_computation.8 | async-start | bytes 24510464 | tf_op jit(solution)/shard_map/all_gather | solution.py:184
  11.9 1429.1 %reduce-scatter.5.cloned.1.call-start = ((), (), s32[]{:S(2)}) async-start(), calls=%async_computation.10 | async-start | bytes 24510464 | tf_op jit(solution)/shard_map/reduce_scatter | solution.py:232
  72.4 90.9 %copy-start.55 = (f32[192]{0:T(256)}, f32[192]{0:T(256)S(1)}, u32[]{:S(2)}) copy-start(f32[192]{0:T(256)S(1)} %add_convert_fusion) | copy-start | bytes 2308
  72.6 90.6 %copy-start.45 = (f32[192]{0:T(256)}, f32[192]{0:T(256)S(1)}, u32[]{:S(2)}) copy-start(f32[192]{0:T(256)S(1)} %add_rsqrt_fusion.2) | copy-start | bytes 2308
  175.9 6.0 copy-start.20
  181.9 4.3 copy-start.25
  199.2 39.4 %copy-start.46 = (f32[192]{0:T(256)S(1)}, f32[192]{0:T(256)}, u32[]{:S(2)}) copy-start(f32[192]{0:T(256)} %copy-done.45) | copy-start | bytes 2308
  313.8 7.2 copy-start.44
  672.8 17.4 copy-start.32
  701.0 1579.8 %reduce-scatter.3.cloned.1.call-start = ((), (), s32[]{:S(2)}) async-start(), calls=%async_computation.9 | async-start | bytes 85229568 | tf_op jit(solution)/shard_map/reduce_scatter | solution.py:229
  745.3 12.2 copy-start.14
  774.1 108.3 %copy-start.4 = (f32[192,2048]{1,0:T(8,128)}, f32[192,2048]{1,0:T(8,128)S(1)}, u32[]{:S(2)}) copy-start(f32[192,2048]{1,0:T(8,128)S(1)} %multiply_add_fusion) | copy-start | bytes 4718596
  791.5 8.7 copy-start.27
  819.1 5.8 copy-start.26
  823.0 7.7 copy-start.54
  846.9 16.1 copy-start.56
  863.0 10.9 slice-start
  867.1 6.8 copy-start.23
  867.1 6.8 slice-start.1
  867.2 9.7 slice-start.2
  877.0 5.4 copy-start.34
  888.2 12.5 copy-start.22
  888.2 12.5 copy-start.24
  913.0 20.9 copy-start.36
  913.0 20.9 copy-start.37
  913.0 20.9 copy-start.38
  1091.8 1348.3 %all-reduce.33.cloned.1.call-start = ((), (), s32[]{:S(2)}) async-start(), calls=%async_computation.11 | async-start | bytes 12910592 | tf_op jit(solution)/shard_map/psum | solution.py:236
  1093.1 3.2 collective-permute-start
  1098.1 64.7 %collective-permute-start.1 = (bf16[2,352,2048]{2,1,0:T(8,128)(2,1)S(1)}, bf16[2,352,2048]{2,1,0:T(8,128)(2,1)}, u32[]{:S(2)}, u32[]{:S(2)}) collective-permute-start(bf16[2,352,2048]{2,1,0:T(8,128)(2,1)S(1)} %pad_maximum_fusion.3), channel_id=1, source_target_pairs={{0,2},{1,3},{2,0},{3,1},{4,6},{5,7},{6,4},{7,5},{8,10},{9,11},{10,... | collective-permute-start | bytes 8650760 | tf_op jit(solution)/shard_map/ppermute | solution.py:22
  1167.2 5.0 copy-start.3
  1172.2 253.3 %collective-permute-start.2 = (bf16[4,352,2048]{2,1,0:T(8,128)(2,1)}, bf16[4,352,2048]{2,1,0:T(8,128)(2,1)}, u32[]{:S(2)}, u32[]{:S(2)}) collective-permute-start(bf16[4,352,2048]{2,1,0:T(8,128)(2,1)} %pad_maximum_fusion.2), channel_id=1, source_target_pairs={{0,4},{1,5},{2,6},{3,7},{4,0},{5,1},{6,2},{7,3},{8,12},{9,13},{10,... | collective-permute-start | bytes 17301512 | tf_op jit(solution)/shard_map/ppermute | solution.py:22
  1429.8 6.8 copy-start
  1429.8 7.8 copy-start.1
  1437.6 843.2 %collective-permute-start.3 = (bf16[8,352,2048]{2,1,0:T(8,128)(2,1)}, bf16[8,352,2048]{2,1,0:T(8,128)(2,1)}, u32[]{:S(2)}, u32[]{:S(2)}) collective-permute-start(bf16[8,352,2048]{2,1,0:T(8,128)(2,1)} %pad_maximum_fusion.1), channel_id=1, source_target_pairs={{0,8},{1,9},{2,10},{3,11},{4,12},{5,13},{6,14},{7,15},{8,0},{9,1},... | collective-permute-start | bytes 34603016 | tf_op jit(solution)/shard_map/ppermute | solution.py:22
  2297.8 20.8 copy-start.5
  2297.8 20.8 copy-start.10
  2297.8 20.8 copy-start.16
  2440.0 3.9 copy-start.2
  (31 other events, 54.1 us)
Sparse Core Ops, SparseCore 0:
  10.2 77.6 all-gather.10
  90.1 73.1 all-gather.12
  165.4 73.1 all-gather.14
  240.6 73.1 all-gather.16
  315.3 116.9 all-gather.20
  433.7 118.6 all-gather.18
  554.0 118.6 all-gather.22
  701.1 226.8 reduce-scatter.4
  1091.9 1188.7 reduce-scatter.2
  2283.1 156.8 all-reduce.32
